TPU v7x, 32 devices: a whole 2x2x4 slice. The times are simulated.
32 devices in a mesh: wide: 4 (over z), step: 2 (over x), img: 4 (over y, core).
Axes of the slice: x: 2, y: 2, z: 4, core: 2. Of those that a mesh axis runs over, the one named last changes fastest.
Arguments:
- activations: bfloat16 [2, 8, 4096, 2560], P('step', 'img', 'wide'), may hold values from -6 to 6
- cotangents: bfloat16 [2, 8, 4096, 10240], P('step', 'img', 'wide'), may hold values from -6 to 6
- projection: bfloat16 [2560, 512], P('wide'), may hold values from -0.125 to 0.125
- buckets: int32 [10240], replicated, may hold values from 0 to 63
- sign_bits: int32 [10240], replicated, may hold values from 0 to 1
- timesteps: int32 [2, 8], P('step', 'img'), may hold values from 0 to 999
Outputs:
- sketch: float32 [8, 32768], P('img', ('wide', 'step'))
Inputs may be any that keep to these rules, and one draw needn't show every extreme that they name: `buckets`: every hidden unit has one bucket.
All inputs are finite; a program needn't handle non-finite values.
Results may differ from a plain program's by a relative error of at most 0.003.
Values may be sent and summed in bfloat16 or wider, within the bound.
No kernel may reach another device: no remote copies, remote signals or barrier semaphores. Data moves between devices by JAX's collectives and lax.ppermute only.
A program may use at most 320 MiB of HBM per device.

v0:
```python
import jax
import jax.numpy as jnp
from jax import lax
from jax.sharding import PartitionSpec as P

RW = 512
KB = 64
DIFF_STEPS = 1000


def local(activations, cotangents, projection, buckets, sign_bits, timesteps):
    image_count = activations.shape[1]
    projected = jnp.einsum(
        "sipd,dr->sipr",
        activations,
        lax.all_gather(projection, "wide", axis=0, tiled=True),
        preferred_element_type=jnp.float32,
    ).astype(jnp.bfloat16)
    weight = 2.0 - 1.5 * timesteps.astype(jnp.float32) / DIFF_STEPS
    sign_vals = (2 * sign_bits - 1).astype(jnp.float32)
    bucket_ids = jnp.arange(KB, dtype=jnp.int32)
    columns = lax.all_to_all(cotangents, "wide", split_axis=3, concat_axis=2, tiled=True)
    col_count = columns.shape[3]
    col_grads = jnp.einsum(
        "sipc,sipr->sicr",
        columns,
        lax.all_gather(projected, "wide", axis=2, tiled=True),
        preferred_element_type=jnp.float32,
    )
    unit = col_grads * lax.rsqrt(jnp.sum(col_grads * col_grads, axis=3, keepdims=True) + 1e-06)
    col_start = lax.axis_index("wide") * col_count
    local_buckets = lax.dynamic_slice_in_dim(buckets, col_start, col_count, 0)
    local_signs = lax.dynamic_slice_in_dim(sign_vals, col_start, col_count, 0)
    bucket_table = jnp.where(
        local_buckets[:, None] == bucket_ids[None, :], local_signs[:, None], 0.0
    )
    sketch_part = jnp.einsum("ck,sicr->sikr", bucket_table, unit, precision=lax.Precision.HIGHEST)
    scaled = sketch_part * weight[:, :, None, None]
    partial_terms = jnp.sum(scaled, axis=0).reshape(image_count, KB * RW)
    return lax.psum_scatter(partial_terms, ("wide", "step"), scatter_dimension=1, tiled=True)


def solution(mesh):
    in_specs = (
        P("step", "img", "wide", None),
        P("step", "img", "wide", None),
        P("wide", None),
        P(),
        P(),
        P("step", "img"),
    )
    out_specs = P("img", ("wide", "step"))
    return jax.shard_map(local, mesh=mesh, in_specs=in_specs, out_specs=out_specs, check_vma=False)
```

profile of v0, /device:TPU:0, one launch (start us, length us, event | category | flops | bytes accessed | tf_op | source)
XLA Modules:
  0.0 1637.5 jit_solution(14158558723203348897)
XLA Ops:
  6.5 102.0 %copy.9 = bf16[1,2,1024,10240]{2,1,0,3:T(2,128)(2,1)} copy(bf16[1,2,1024,10240]{3,2,1,0:T(8,128)(2,1)} %param.7) | data formatting | bytes 83886080 | tf_op args[1]
  108.5 11.2 all-to-all-start
  119.7 0.0 all-gather.4.cloned.1.call-start
  119.7 0.7 all-gather.4.cloned.1.call-update
  120.4 0.0 copy-start
  120.4 0.0 all-gather.6.cloned.1.call-start
  120.5 293.3 %all-gather.4.cloned.1.call-done = bf16[2560,512]{1,0:T(8,128)(2,1)} async-done(((bf16[640,512]{1,0:T(8,128)(2,1)}), bf16[2560,512]{1,0:T(8,128)(2,1)}) %all-gather.4.cloned.1.call-update) | async-done | bytes 2621456 | tf_op jit(solution)/shard_map/all_gather | solution.py:16
  413.8 10.2 fusion.7
  424.0 0.0 all-gather.6.cloned.1.call-update
  424.0 0.0 reduce-scatter.4.cloned.1.call-start
  424.1 0.8 dynamic_slice.6
  424.9 0.8 fusion.27
  425.7 0.0 copy-done
  425.7 774.8 %all-to-all-done = bf16[1,2,1024,10240]{2,1,0,3:T(2,128)(2,1)} async-done(((bf16[1,2,1024,10240]{2,1,0,3:T(2,128)(2,1)}), bf16[1,2,1024,10240]{2,1,0,3:T(2,128)(2,1)}, u32[]{:S(2)}, u32[]{:S(2)}) %all-to-all-start) | async-done | bytes 41943072 | tf_op jit(solution)/shard_map/all_to_all | solution.py:22
  1200.5 101.1 %copy.10 = bf16[1,2,1024,4,2560]{4,2,3,1,0:T(8,128)(2,1)} copy(bf16[1,2,1024,4,2560]{2,1,4,3,0:T(2,128)(2,1)} %bitcast.2) | data formatting | bytes 83886080 | tf_op jit(solution)/shard_map/all_to_all | solution.py:22
  1301.6 0.0 all-gather.6.cloned.1.call-done
  1301.6 27.9 %multiply_reduce_fusion = (f32[2,2560]{1,0:T(2,128)S(1)}, f32[2,512,2560]{2,1,0:T(8,128)S(1)}) fusion(bf16[2,4096,512]{1,2,0:T(8,128)(2,1)} %all-gather.6.cloned.1.call-done, bf16[2,4096,2560]{2,1,0:T(8,128)(2,1)} %bitcast.43), kind=kOutput, calls=%fused_computation.5 | convolution fusion | flops 21480075264 | bytes 60837888 | tf_op jit(solution)/shard_map/sipc,sipr->sicr/dot_general | solution.py:24
  1329.5 10.6 fusion.18
  1340.1 8.6 copy.15
  1348.6 0.0 reduce-scatter.4.cloned.1.call-update
  1348.7 279.5 %reduce-scatter.4.cloned.1.call-done = f32[4096,2]{1,0:T(8,128)} async-done(((f32[32768,2]{1,0:T(8,128)}), f32[4096,2]{1,0:T(8,128)}) %reduce-scatter.4.cloned.1.call-update) | async-done | bytes 32784
  1628.2 2.8 copy.14
  (2 shorter events, 0.0 us)
Async XLA Ops:
  108.5 1092.0 %all-to-all-start = ((bf16[1,2,1024,10240]{2,1,0,3:T(2,128)(2,1)}), bf16[1,2,1024,10240]{2,1,0,3:T(2,128)(2,1)}, u32[]{:S(2)}, u32[]{:S(2)}) async-start(bf16[1,2,1024,10240]{2,1,0,3:T(2,128)(2,1)} %copy.9), calls=%async_computation | async-start | bytes 83886080 | tf_op jit(solution)/shard_map/all_to_all | solution.py:22
  119.7 294.1 %all-gather.4.cloned.1.call-start = ((), (), s32[]{:S(2)}) async-start(), calls=%async_computation.2 | async-start | bytes 3276800 | tf_op jit(solution)/shard_map/all_gather | solution.py:16
  120.4 305.3 %copy-start = (s32[1,2]{1,0:T(1,128)S(1)}, s32[1,2]{1,0:T(1,128)}, u32[]{:S(2)}) copy-start(s32[1,2]{1,0:T(1,128)} %param.11) | copy-start | bytes 28
  120.4 1181.1 %all-gather.6.cloned.1.call-start = ((), (), s32[]{:S(2)}) async-start(), calls=%async_computation.3 | async-start | bytes 10485760 | tf_op jit(solution)/shard_map/all_gather | solution.py:27
  424.0 1204.1 %reduce-scatter.4.cloned.1.call-start = ((), (), s32[]{:S(2)}) async-start(), calls=%async_computation.4 | async-start | bytes 18874368
Sparse Core Ops, SparseCore 0:
  122.1 291.7 all-gather.3
  424.2 278.0 all-gather.5
  1348.8 279.3 reduce-scatter.3
where the time goes:
time: 1640 us
  waiting for transfers between devices  1350 us (82%)
  local copies, waits for them, and re-layouts  215 us (13%)
  matrix products  48.7 us (3%)
    all_to_all x1, waiting for transfers between devices, local(): lax.all_to_all(cotangents, 'wide', split_axis=3, concat_axis=2, tiled=True)  775 us
    all_gather x1, waiting for transfers between devices, local(): lax.all_gather(projection, 'wide', axis=0, tiled=True)  293 us
    unnamed x4, waiting for transfers between devices  280 us
    unnamed x5, local copies, waits for them, and re-layouts  113 us
    all_to_all x1, local copies, waits for them, and re-layouts, local(): lax.all_to_all(cotangents, 'wide', split_axis=3, concat_axis=2, tiled=True)  101 us
  transfers between devices with their start and end apart: 4, of which 3 were waited for; matrix products, arithmetic and copies ran while one was open for 7% of the time, Pallas kernels for 0%

commit v1 on v0

--- a/solution.py
+++ b/solution.py
@@ -19,7 +19,12 @@
     weight = 2.0 - 1.5 * timesteps.astype(jnp.float32) / DIFF_STEPS
     sign_vals = (2 * sign_bits - 1).astype(jnp.float32)
     bucket_ids = jnp.arange(KB, dtype=jnp.int32)
-    columns = lax.all_to_all(cotangents, "wide", split_axis=3, concat_axis=2, tiled=True)
+    columns = jnp.concatenate(
+        lax.all_to_all(
+            jnp.stack(jnp.split(cotangents, lax.axis_size("wide"), axis=3)), "wide", 0, 0
+        ),
+        axis=2,
+    )
     col_count = columns.shape[3]
     col_grads = jnp.einsum(
         "sipc,sipr->sicr",

time: 1640 us -> 1520 us (0.927)
  local copies, waits for them, and re-layouts: 215 us -> 69.3 us
  other arithmetic: 0.82 us -> 29.4 us
    unnamed x5 -> x4, local copies, waits for them, and re-layouts: 113 us -> 11.4 us
    all_to_all x1 -> x0, local copies, waits for them, and re-layouts: 101 us -> none  [local(): lax.all_to_all(cotangents, 'wide', split_axis=3, concat_axis=2, tiled=True)]
    another operation x0 -> x1, local copies, waits for them, and re-layouts: none -> 28.7 us  [local(): jnp.stack(jnp.split(cotangents, lax.axis_size('wide'), axis=3))]
    another operation x0 -> x1, other arithmetic: none -> 28.6 us  [local(): jnp.stack(jnp.split(cotangents, lax.axis_size('wide'), axis=3))]
    reshape x0 -> x1, local copies, waits for them, and re-layouts: none -> 28.4 us  [local(): jnp.concatenate(lax.all_to_all(jnp.stack(jnp.split(cotangents, lax.axis_s...]
  transfers between devices with their start and end apart: 4 -> 4, of which waited for: 3 -> 3; matrix products, arithmetic and copies ran while one was open for 7% -> 3% of each run, Pallas kernels for 0% -> 0%
where the time goes in v1:
time: 1520 us
  waiting for transfers between devices  1350 us (89%)
  local copies, waits for them, and re-layouts  69.3 us (5%)
  matrix products  48.7 us (3%)
  other arithmetic  29.4 us (2%)
    all_to_all x1, waiting for transfers between devices, local(): lax.all_to_all(jnp.stack(jnp.split(cotangents, lax.axis_size('wide'), axi...  775 us
    all_gather x1, waiting for transfers between devices, local(): lax.all_gather(projection, 'wide', axis=0, tiled=True)  293 us
    unnamed x4, waiting for transfers between devices  280 us
  transfers between devices with their start and end apart: 4, of which 3 were waited for; matrix products, arithmetic and copies ran while one was open for 3% of the time, Pallas kernels for 0%

profile of v1, /device:TPU:0, one launch (start us, length us, event | category | flops | bytes accessed | tf_op | source)
XLA Modules:
  0.0 1520.1 jit_solution(10425926994783141363)
XLA Ops:
  6.5 28.7 %slice_bitcast_fusion.3 = (bf16[1,1,2,1024,2560]{4,3,2,1,0:T(8,128)(2,1)}, bf16[1,1,2,1024,2560]{4,3,2,1,0:T(8,128)(2,1)}, bf16[1,1,2,1024,2560]{4,3,2,1,0:T(8,128)(2,1)}, bf16[1,1,2,1024,2560]{4,3,2,1,0:T(8,128)(2,1)}) fusion(bf16[1,2,1024,10240]{3,2,1,0:T(8,128)(2,1)} %param.7), kind=kLoop, calls=%fused_computation.9 | loop fusion | bytes 83886080 | tf_op jit(solution)/shard_map/stack | solution.py:24
  35.2 28.6 %pad_maximum_fusion = bf16[4,1,2,1024,2560]{4,3,2,1,0:T(8,128)(2,1)} fusion(bf16[1,1,2,1024,2560]{4,3,2,1,0:T(8,128)(2,1)} %get-tuple-element.7, bf16[1,1,2,1024,2560]{4,3,2,1,0:T(8,128)(2,1)} %get-tuple-element.8, bf16[1,1,2,1024,2560]{4,3,2,1,0:T(8,128)(2,1)} %get-tuple-element.6, bf16[1,1,2,1024,2560]{4,3,2,1,0:T(8,128)(2,1)} %get-tuple-element.5), kind=kLoop, calls=%fused_computation | loop fusion | flops 62914560 | bytes 83886080 | tf_op jit(solution)/shard_map/stack | solution.py:24
  63.8 11.2 all-to-all-start
  75.0 0.0 all-gather.4.cloned.1.call-start
  75.0 0.7 all-gather.4.cloned.1.call-update
  75.7 0.0 copy-start
  75.7 0.0 all-gather.6.cloned.1.call-start
  75.8 293.5 %all-gather.4.cloned.1.call-done = bf16[2560,512]{1,0:T(8,128)(2,1)} async-done(((bf16[640,512]{1,0:T(8,128)(2,1)}), bf16[2560,512]{1,0:T(8,128)(2,1)}) %all-gather.4.cloned.1.call-update) | async-done | bytes 2621456 | tf_op jit(solution)/shard_map/all_gather | solution.py:16
  369.3 10.2 fusion.6
  379.4 0.0 all-gather.6.cloned.1.call-update
  379.5 0.0 reduce-scatter.4.cloned.1.call-start
  379.5 0.8 dynamic_slice.6
  380.3 0.8 fusion.26
  381.1 0.0 copy-done
  381.1 774.7 %all-to-all-done = bf16[4,1,2,1024,2560]{4,3,2,1,0:T(8,128)(2,1)} async-done(((bf16[4,1,2,1024,2560]{4,3,2,1,0:T(8,128)(2,1)}), bf16[4,1,2,1024,2560]{4,3,2,1,0:T(8,128)(2,1)}, u32[]{:S(2)}, u32[]{:S(2)}) %all-to-all-start) | async-done | bytes 41943072 | tf_op jit(solution)/shard_map/all_to_all | solution.py:23
  1155.8 28.4 %copy.9 = bf16[1,2,4,1024,2560]{4,3,2,1,0:T(8,128)(2,1)} copy(bf16[1,2,4,1024,2560]{4,3,1,0,2:T(8,128)(2,1)} %bitcast.4) | data formatting | bytes 83886080 | tf_op jit(solution)/shard_map/reshape | solution.py:22
  1184.3 0.0 all-gather.6.cloned.1.call-done
  1184.3 27.9 %multiply_reduce_fusion = (f32[2,2560]{1,0:T(2,128)S(1)}, f32[2,2560,512]{1,2,0:T(8,128)S(1)}) fusion(bf16[2,4096,512]{1,2,0:T(8,128)(2,1)} %all-gather.6.cloned.1.call-done, bf16[2,4096,2560]{2,1,0:T(8,128)(2,1)} %bitcast.40), kind=kOutput, calls=%fused_computation.5 | convolution fusion | flops 21480075264 | bytes 60837888 | tf_op jit(solution)/shard_map/sipc,sipr->sicr/dot_general | solution.py:29
  1212.2 10.6 fusion.17
  1222.8 8.6 copy.14
  1231.3 0.0 reduce-scatter.4.cloned.1.call-update
  1231.4 279.4 %reduce-scatter.4.cloned.1.call-done = f32[4096,2]{1,0:T(8,128)} async-done(((f32[32768,2]{1,0:T(8,128)}), f32[4096,2]{1,0:T(8,128)}) %reduce-scatter.4.cloned.1.call-update) | async-done | bytes 32784
  1510.8 2.8 copy.13
  (2 shorter events, 0.0 us)
Async XLA Ops:
  63.8 1092.0 %all-to-all-start = ((bf16[4,1,2,1024,2560]{4,3,2,1,0:T(8,128)(2,1)}), bf16[4,1,2,1024,2560]{4,3,2,1,0:T(8,128)(2,1)}, u32[]{:S(2)}, u32[]{:S(2)}) async-start(bf16[4,1,2,1024,2560]{4,3,2,1,0:T(8,128)(2,1)} %pad_maximum_fusion), calls=%async_computation | async-start | bytes 83886080 | tf_op jit(solution)/shard_map/all_to_all | solution.py:23
  75.0 294.3 %all-gather.4.cloned.1.call-start = ((), (), s32[]{:S(2)}) async-start(), calls=%async_computation.2 | async-start | bytes 3276800 | tf_op jit(solution)/shard_map/all_gather | solution.py:16
  75.7 305.4 %copy-start = (s32[1,2]{1,0:T(1,128)S(1)}, s32[1,2]{1,0:T(1,128)}, u32[]{:S(2)}) copy-start(s32[1,2]{1,0:T(1,128)} %param.11) | copy-start | bytes 28
  75.7 1108.5 %all-gather.6.cloned.1.call-start = ((), (), s32[]{:S(2)}) async-start(), calls=%async_computation.3 | async-start | bytes 10485760 | tf_op jit(solution)/shard_map/all_gather | solution.py:32
  379.5 1131.3 %reduce-scatter.4.cloned.1.call-start = ((), (), s32[]{:S(2)}) async-start(), calls=%async_computation.4 | async-start | bytes 18874368
Sparse Core Ops, SparseCore 0:
  77.4 291.8 all-gather.3
  379.6 277.9 all-gather.5
  1231.5 279.2 reduce-scatter.3
